TPU v7x, 32 devices: a whole 2x2x4 slice. The times are simulated.
32 devices in a mesh: dp: 2 (over core), blk: 4 (over y, x), rep: 4 (over z).
Axes of the slice: x: 2, y: 2, z: 4, core: 2. Of those that a mesh axis runs over, the one named last changes fastest.
Arguments:
- feats: bfloat16 [2, 16384, 512], P('dp', ('blk', 'rep')), may hold values from -6 to 6
- weight: bfloat16 [512, 512], replicated, may hold values from -0.25 to 0.25
- cols: int32 [2, 128, 15], P('dp', ('blk', 'rep')), may hold values from -1 to 127, as said below
- vals: bfloat16 [2, 128, 15, 128, 128], P('dp', ('blk', 'rep')), as said below
- cotangent: bfloat16 [2, 16384, 512], P('dp', ('blk', 'rep')), may hold values from -6 to 6
Outputs:
- activ: bfloat16 [2, 16384, 512], P('dp', ('blk', 'rep'))
- feat_grad: bfloat16 [2, 16384, 512], P('dp', ('blk', 'rep'))
- weight_grad: float32 [512, 512], replicated
Inputs may be any that keep to these rules, and one draw needn't show every extreme that they name: `cols`: used slots come first in each row and -1 marks the unused ones. Slot 0 of block row p names p itself; every other used slot names a block at most 7 away from p, each at most once. The relation is symmetric: p names q exactly when q names p. In every scenario some block row uses all 15 slots. `vals`: the block in row p's slot naming q is the transpose of the block in row q's slot naming p (the self block is symmetric); unused slots hold zeros.
All inputs are finite; a program needn't handle non-finite values.
Results may differ from a plain program's by a relative error of at most 0.0061.
Values may be sent and summed in bfloat16 or wider, within the bound.
No kernel may reach another device: no remote copies, remote signals or barrier semaphores. Data moves between devices by JAX's collectives and lax.ppermute only.
A program may use at most 128 MiB of HBM per device.

v0:
```python
import jax
import jax.numpy as jnp
from jax import lax
from jax.sharding import PartitionSpec as P

REACH = 7


def padded(cells, sides, width):
    for axis, dim in sides:
        count = lax.axis_size(axis)
        ends = count - 1
        head = lax.slice_in_dim(cells, 0, width, axis=dim)
        tail = lax.slice_in_dim(cells, cells.shape[dim] - width, cells.shape[dim], axis=dim)
        cells = jnp.concatenate(
            [
                lax.ppermute(tail, axis, [(i, (i + 1) % count) for i in range(ends)]),
                cells,
                lax.ppermute(head, axis, [((i + 1) % count, i) for i in range(ends)]),
            ],
            axis=dim,
        )
    return cells


def spread(extended, row_cols, row_vals, first):
    row_blocks = row_vals.shape[0]
    block_size = row_vals.shape[2]
    width = extended.shape[1]
    ext_blocks = extended.reshape(-1, block_size, width)
    margin = (ext_blocks.shape[0] - row_blocks) // 2
    local_index = jnp.where(row_cols >= 0, row_cols - first + margin, 0)
    picked = ext_blocks[local_index]
    summed = jnp.einsum("rkab,rkbf->raf", row_vals, picked, preferred_element_type=jnp.float32)
    return summed.reshape(-1, width)


def shards(feats, weight, cols, vals, cotangent):
    first = lax.axis_index(("blk", "rep")) * cols.shape[1]
    rim_rows = REACH * vals.shape[3]
    own = feats[0]
    projected = jnp.dot(own, weight, preferred_element_type=jnp.float32).astype(jnp.bfloat16)
    extended = padded(projected, ((("blk", "rep"), 0),), rim_rows)
    agg = spread(extended, cols[0], vals[0], first)
    sig = jax.nn.sigmoid(agg)
    activ_list = [(agg * sig).astype(jnp.bfloat16)]
    dagg = (cotangent[0].astype(jnp.float32) * sig * (1.0 + agg * (1.0 - sig))).astype(jnp.bfloat16)
    grad_ext = padded(dagg, ((("blk", "rep"), 0),), rim_rows)
    dproj = spread(grad_ext, cols[0], vals[0], first).astype(jnp.bfloat16)
    back = lax.dot_general(
        dproj, weight, (((1,), (1,)), ((), ())), preferred_element_type=jnp.float32
    )
    grad_list = [back.astype(jnp.bfloat16)]
    grads = lax.dot_general(
        own, dproj, (((0,), (0,)), ((), ())), preferred_element_type=jnp.float32
    )
    weight_grad = lax.psum(grads, ("dp", "blk", "rep"))
    return (jnp.stack(activ_list), jnp.stack(grad_list), weight_grad)


def solution(mesh):
    placed = (
        P("dp", ("blk", "rep"), None),
        P(),
        P("dp", ("blk", "rep"), None),
        P("dp", ("blk", "rep"), None, None, None),
        P("dp", ("blk", "rep"), None),
    )
    return jax.shard_map(
        shards,
        mesh=mesh,
        in_specs=placed,
        out_specs=(P("dp", ("blk", "rep"), None), P("dp", ("blk", "rep"), None), P()),
        check_vma=False,
    )
```

profile of v0, /device:TPU:0, one launch (start us, length us, event | category | flops | bytes accessed | tf_op | source)
XLA Modules:
  0.0 287.8 jit_solution(11901660477694064899)
XLA Ops:
  7.2 0.0 copy-start
  7.2 0.0 copy-start.4
  7.2 0.0 all-reduce.2.cloned.1.call-start
  7.2 1.2 copy-done
  8.4 1.7 convolution_convert_fusion.1
  10.1 1.1 fusion.16
  11.2 5.9 %collective-permute-start = (bf16[896,512]{1,0:T(8,128)(2,1)}, bf16[896,512]{1,0:T(8,128)(2,1)}, u32[]{:S(2)}, u32[]{:S(2)}) collective-permute-start(bf16[896,512]{1,0:T(8,128)(2,1)} %get-tuple-element.8), channel_id=1, source_target_pairs={{0,1},{1,2},{2,3},{3,4},{4,5},{5,6},{6,7},{7,8},{8,9},{9,10},{10,1... | collective-permute-start | bytes 2752520 | tf_op jit(solution)/shard_map/ppermute | solution.py:17
  17.1 1.3 collective-permute-start.1
  18.4 0.0 copy-done.4
  18.4 0.1 reshape.102
  18.5 17.5 %collective-permute-done = bf16[896,512]{1,0:T(8,128)(2,1)} collective-permute-done((bf16[896,512]{1,0:T(8,128)(2,1)}, bf16[896,512]{1,0:T(8,128)(2,1)}, u32[]{:S(2)}, u32[]{:S(2)}) %collective-permute-start) | collective-permute-done | bytes 917536 | tf_op jit(solution)/shard_map/ppermute | solution.py:17
  36.1 23.3 %collective-permute-done.1 = bf16[896,512]{1,0:T(8,128)(2,1)} collective-permute-done((bf16[896,512]{1,0:T(8,128)(2,1)S(1)}, bf16[896,512]{1,0:T(8,128)(2,1)}, u32[]{:S(2)}, u32[]{:S(2)}) %collective-permute-start.1) | collective-permute-done | bytes 917536 | tf_op jit(solution)/shard_map/ppermute | solution.py:19
  59.3 3.2 %pad_maximum_fusion = bf16[2816,512]{1,0:T(8,128)(2,1)} fusion(bf16[896,512]{1,0:T(8,128)(2,1)} %collective-permute-done.1, bf16[1024,512]{1,0:T(8,128)(2,1)S(1)} %convolution_convert_fusion.1, bf16[896,512]{1,0:T(8,128)(2,1)} %collective-permute-done), kind=kLoop, calls=%fused_computation.6 | loop fusion | flops 8650752 | bytes 5767168 | tf_op jit(solution)/shard_map/concatenate | solution.py:15
  62.6 9.5 %gather_fusion = bf16[120,128,512]{2,1,0:T(8,128)(2,1)} fusion(bf16[22,128,512]{2,1,0:T(8,128)(2,1)} %bitcast.62, s32[1024]{0:T(1024)S(1)} %pad_clamp_fusion), kind=kCustom, calls=%fused_computation | custom fusion | bytes 31457760 | tf_op jit(solution)/shard_map/gather | solution.py:33
  72.1 0.0 copy-start.3
  72.1 8.2 %fusion = f32[8,512,128,1]{1,2,3,0:T(8,128)S(1)} fusion(bf16[8,15,128,512]{3,2,1,0:T(8,128)(2,1)} %bitcast.64, bf16[1,8,15,128,128]{4,3,2,1,0:T(8,128)(2,1)} %param.8), kind=kOutput, calls=%fused_computation.2 | convolution fusion | flops 2013265920 | bytes 21757952 | tf_op jit(solution)/shard_map/rkab,rkbf->raf/dot_general | solution.py:34
  80.3 0.0 copy-done.3
  80.3 0.8 fusion.5
  81.1 0.1 fusion.15
  81.3 2.5 collective-permute-start.2
  83.8 1.3 collective-permute-start.3
  85.1 18.4 %collective-permute-done.2 = bf16[896,512]{1,0:T(8,128)(2,1)S(1)} collective-permute-done((bf16[896,512]{1,0:T(8,128)(2,1)S(1)}, bf16[896,512]{1,0:T(8,128)(2,1)S(1)}, u32[]{:S(2)}, u32[]{:S(2)}) %collective-permute-start.2) | collective-permute-done | bytes 917536 | tf_op jit(solution)/shard_map/ppermute | solution.py:17
  103.5 23.8 %collective-permute-done.3 = bf16[896,512]{1,0:T(8,128)(2,1)S(1)} collective-permute-done((bf16[896,512]{1,0:T(8,128)(2,1)S(1)}, bf16[896,512]{1,0:T(8,128)(2,1)S(1)}, u32[]{:S(2)}, u32[]{:S(2)}) %collective-permute-start.3) | collective-permute-done | bytes 917536 | tf_op jit(solution)/shard_map/ppermute | solution.py:19
  127.3 1.8 pad_maximum_fusion.1
  129.1 9.5 %gather_fusion.1 = bf16[120,128,512]{2,1,0:T(8,128)(2,1)} fusion(bf16[22,128,512]{2,1,0:T(8,128)(2,1)} %bitcast.61, s32[1024]{0:T(1024)S(1)} %pad_clamp_fusion), kind=kCustom, calls=%fused_computation.1 | custom fusion | bytes 31457760 | tf_op jit(solution)/shard_map/gather | solution.py:33
  138.6 9.0 %bitcast_convert_fusion = bf16[8,512,128]{1,2,0:T(8,128)(2,1)S(1)} fusion(bf16[8,15,128,512]{3,2,1,0:T(8,128)(2,1)} %bitcast.63, bf16[1,8,15,128,128]{4,3,2,1,0:T(8,128)(2,1)} %param.8), kind=kOutput, calls=%fused_computation.11 | convolution fusion | flops 2013790208 | bytes 20709376 | tf_op jit(solution)/shard_map/rkab,rkbf->raf/dot_general | solution.py:34
  147.6 0.0 copy-start.1
  147.7 1.0 copy-done.1
  148.6 1.7 convolution_bitcast_fusion
  150.4 0.0 all-reduce.2.cloned.1.call-update
  150.4 0.0 copy-start.2
  150.4 0.0 copy-start.5
  150.4 1.5 multiply_convert_fusion
  151.9 0.0 copy-done.2
  151.9 0.0 copy-done.5
  151.9 1.7 fusion.12
  153.6 124.8 %all-reduce.2.cloned.1.call-done = f32[512,512]{0,1:T(8,128)} async-done(((f32[512,512]{0,1:T(8,128)}), f32[512,512]{0,1:T(8,128)}) %all-reduce.2.cloned.1.call-update) | async-done | bytes 1048592 | tf_op jit(solution)/shard_map/psum | solution.py:57
  278.4 2.5 copy.8
  (2 shorter events, 0.0 us)
Async XLA Ops:
  7.2 1.2 copy-start
  7.2 11.2 %copy-start.4 = (s32[1,8,15]{2,1,0:T(8,128)S(1)}, s32[1,8,15]{2,1,0:T(8,128)}, u32[]{:S(2)}) copy-start(s32[1,8,15]{2,1,0:T(8,128)} %param.7) | copy-start | bytes 1444
  7.2 271.2 %all-reduce.2.cloned.1.call-start = ((), (), s32[]{:S(2)}) async-start(), calls=%async_computation | async-start | bytes 2097152 | tf_op jit(solution)/shard_map/psum | solution.py:57
  11.2 24.8 %collective-permute-start = (bf16[896,512]{1,0:T(8,128)(2,1)}, bf16[896,512]{1,0:T(8,128)(2,1)}, u32[]{:S(2)}, u32[]{:S(2)}) collective-permute-start(bf16[896,512]{1,0:T(8,128)(2,1)} %get-tuple-element.8), channel_id=1, source_target_pairs={{0,1},{1,2},{2,3},{3,4},{4,5},{5,6},{6,7},{7,8},{8,9},{9,10},{10,1... | collective-permute-start | bytes 2752520 | tf_op jit(solution)/shard_map/ppermute | solution.py:17
  17.1 42.2 %collective-permute-start.1 = (bf16[896,512]{1,0:T(8,128)(2,1)S(1)}, bf16[896,512]{1,0:T(8,128)(2,1)}, u32[]{:S(2)}, u32[]{:S(2)}) collective-permute-start(bf16[896,512]{1,0:T(8,128)(2,1)S(1)} %get-tuple-element.9), channel_id=1, source_target_pairs={{1,0},{2,1},{3,2},{4,3},{5,4},{6,5},{7,6},{8,7},{9,8},{10,9},{11,1... | collective-permute-start | bytes 2752520 | tf_op jit(solution)/shard_map/ppermute | solution.py:19
  72.1 8.2 %copy-start.3 = (bf16[1,1024,512]{2,1,0:T(8,128)(2,1)S(1)}, bf16[1,1024,512]{2,1,0:T(8,128)(2,1)}, u32[]{:S(2)}) copy-start(bf16[1,1024,512]{2,1,0:T(8,128)(2,1)} %param.9) | copy-start | bytes 3145732
  81.3 22.2 %collective-permute-start.2 = (bf16[896,512]{1,0:T(8,128)(2,1)S(1)}, bf16[896,512]{1,0:T(8,128)(2,1)S(1)}, u32[]{:S(2)}, u32[]{:S(2)}) collective-permute-start(bf16[896,512]{1,0:T(8,128)(2,1)S(1)} %get-tuple-element.6), channel_id=1, source_target_pairs={{0,1},{1,2},{2,3},{3,4},{4,5},{5,6},{6,7},{7,8},{8,9},{9,10},{10,1... | collective-permute-start | bytes 2752520 | tf_op jit(solution)/shard_map/ppermute | solution.py:17
  83.8 43.5 %collective-permute-start.3 = (bf16[896,512]{1,0:T(8,128)(2,1)S(1)}, bf16[896,512]{1,0:T(8,128)(2,1)S(1)}, u32[]{:S(2)}, u32[]{:S(2)}) collective-permute-start(bf16[896,512]{1,0:T(8,128)(2,1)S(1)} %get-tuple-element.7), channel_id=1, source_target_pairs={{1,0},{2,1},{3,2},{4,3},{5,4},{6,5},{7,6},{8,7},{9,8},{10,9},{11,1... | collective-permute-start | bytes 2752520 | tf_op jit(solution)/shard_map/ppermute | solution.py:19
  147.6 1.0 copy-start.1
  150.4 1.5 copy-start.2
  150.4 1.5 copy-start.5
Sparse Core Ops, SparseCore 0:
  150.5 127.8 all-reduce.1
where the time goes:
time: 288 us
  waiting for transfers between devices  208 us (72%)
  local copies, waits for them, and re-layouts  25 us (9%)
  matrix products  22.4 us (8%)
  between operations  14.2 us (5%)
  starting transfers between devices  11 us (4%)
  other arithmetic  7.32 us (3%)
    psum x1, waiting for transfers between devices, shards(): weight_grad = lax.psum(grads, ('dp', 'blk', 'rep'))  125 us
    ppermute x2, waiting for transfers between devices, padded(): lax.ppermute(head, axis, [((i + 1) % count, i) for i in range(ends)])  47.1 us
    ppermute x2, waiting for transfers between devices, padded(): lax.ppermute(tail, axis, [(i, (i + 1) % count) for i in range(ends)])  35.9 us
    gather x2, local copies, waits for them, and re-layouts, spread(): picked = ext_blocks[local_index]  19 us
    dot_general x2, matrix products, spread(): jnp.einsum('rkab,rkbf->raf', row_vals, picked, preferred_element_type=jnp...  17.2 us
    ppermute x2, starting transfers between devices, padded(): lax.ppermute(tail, axis, [(i, (i + 1) % count) for i in range(ends)])  8.42 us
  transfers between devices with their start and end apart: 5, of which 5 were waited for; matrix products, arithmetic and copies ran while one was open for 1% of the time, Pallas kernels for 0%

commit v1 on v0

--- a/solution.py
+++ b/solution.py
@@ -4,6 +4,11 @@
 from jax.sharding import PartitionSpec as P
 
 REACH = 7
+
+
+def summed_here(x, name):
+    parts = lax.all_gather(x, name)
+    return jnp.sum(parts, axis=0)
 
 
 def padded(cells, sides, width):
@@ -54,7 +59,7 @@
     grads = lax.dot_general(
         own, dproj, (((0,), (0,)), ((), ())), preferred_element_type=jnp.float32
     )
-    weight_grad = lax.psum(grads, ("dp", "blk", "rep"))
+    weight_grad = summed_here(grads, ("dp", "blk", "rep"))
     return (jnp.stack(activ_list), jnp.stack(grad_list), weight_grad)
 
 

time: 288 us -> 394 us (1.37)
  waiting for transfers between devices: 208 us -> 277 us
  local copies, waits for them, and re-layouts: 25 us -> 56.3 us
  other arithmetic: 7.32 us -> 12.7 us
    all_gather x0 -> x1, waiting for transfers between devices: none -> 194 us  [summed_here(): parts = lax.all_gather(x, name)]
    psum x1 -> x0, waiting for transfers between devices: 125 us -> none  [shards(): weight_grad = lax.psum(grads, ('dp', 'blk', 'rep'))]
    unnamed x13 -> x16, local copies, waits for them, and re-layouts: 4.68 us -> 36 us
    reduce_sum x0 -> x1, other arithmetic: none -> 5.36 us  [summed_here(): return jnp.sum(parts, axis=0)]
where the time goes in v1:
time: 394 us
  waiting for transfers between devices  277 us (70%)
  local copies, waits for them, and re-layouts  56.3 us (14%)
  matrix products  22.4 us (6%)
  between operations  14.2 us (4%)
  other arithmetic  12.7 us (3%)
  starting transfers between devices  11.2 us (3%)
    all_gather x1, waiting for transfers between devices, summed_here(): parts = lax.all_gather(x, name)  194 us
    ppermute x2, waiting for transfers between devices, padded(): lax.ppermute(head, axis, [((i + 1) % count, i) for i in range(ends)])  47.1 us
    unnamed x16, local copies, waits for them, and re-layouts  36 us
    ppermute x2, waiting for transfers between devices, padded(): lax.ppermute(tail, axis, [(i, (i + 1) % count) for i in range(ends)])  35.7 us
    gather x2, local copies, waits for them, and re-layouts, spread(): picked = ext_blocks[local_index]  19 us
    dot_general x2, matrix products, spread(): jnp.einsum('rkab,rkbf->raf', row_vals, picked, preferred_element_type=jnp...  17.2 us
    ppermute x2, starting transfers between devices, padded(): lax.ppermute(tail, axis, [(i, (i + 1) % count) for i in range(ends)])  8.43 us
  transfers between devices with their start and end apart: 5, of which 5 were waited for; matrix products, arithmetic and copies ran while one was open for 1% of the time, Pallas kernels for 0%

profile of v1, /device:TPU:0, one launch (start us, length us, event | category | flops | bytes accessed | tf_op | source)
XLA Modules:
  0.0 393.6 jit_solution(5051359274626404496)
XLA Ops:
  7.2 0.0 copy-start
  7.2 0.0 copy-start.5
  7.2 0.0 all-gather.3.cloned.1.call-start
  7.2 1.2 copy-done
  8.4 1.7 convolution_convert_fusion.1
  10.1 1.1 fusion.16
  11.2 5.9 %collective-permute-start = (bf16[896,512]{1,0:T(8,128)(2,1)}, bf16[896,512]{1,0:T(8,128)(2,1)}, u32[]{:S(2)}, u32[]{:S(2)}) collective-permute-start(bf16[896,512]{1,0:T(8,128)(2,1)} %get-tuple-element.8), channel_id=1, source_target_pairs={{0,1},{1,2},{2,3},{3,4},{4,5},{5,6},{6,7},{7,8},{8,9},{9,10},{10,1... | collective-permute-start | bytes 2752520 | tf_op jit(solution)/shard_map/ppermute | solution.py:22
  17.1 1.3 collective-permute-start.1
  18.4 0.0 copy-done.5
  18.4 0.1 reshape.102
  18.5 17.5 %collective-permute-done = bf16[896,512]{1,0:T(8,128)(2,1)} collective-permute-done((bf16[896,512]{1,0:T(8,128)(2,1)}, bf16[896,512]{1,0:T(8,128)(2,1)}, u32[]{:S(2)}, u32[]{:S(2)}) %collective-permute-start) | collective-permute-done | bytes 917536 | tf_op jit(solution)/shard_map/ppermute | solution.py:22
  36.0 23.3 %collective-permute-done.1 = bf16[896,512]{1,0:T(8,128)(2,1)} collective-permute-done((bf16[896,512]{1,0:T(8,128)(2,1)S(1)}, bf16[896,512]{1,0:T(8,128)(2,1)}, u32[]{:S(2)}, u32[]{:S(2)}) %collective-permute-start.1) | collective-permute-done | bytes 917536 | tf_op jit(solution)/shard_map/ppermute | solution.py:24
  59.3 3.2 pad_maximum_fusion
  62.6 9.5 %gather_fusion = bf16[120,128,512]{2,1,0:T(8,128)(2,1)} fusion(bf16[22,128,512]{2,1,0:T(8,128)(2,1)} %bitcast.67, s32[1024]{0:T(1024)S(1)} %pad_clamp_fusion), kind=kCustom, calls=%fused_computation | custom fusion | bytes 31457760 | tf_op jit(solution)/shard_map/gather | solution.py:38
  72.1 0.0 copy-start.4
  72.1 8.2 %fusion = f32[8,512,128,1]{1,2,3,0:T(8,128)S(1)} fusion(bf16[8,15,128,512]{3,2,1,0:T(8,128)(2,1)} %bitcast.69, bf16[1,8,15,128,128]{4,3,2,1,0:T(8,128)(2,1)} %param.8), kind=kOutput, calls=%fused_computation.3 | convolution fusion | flops 2013265920 | bytes 21757952 | tf_op jit(solution)/shard_map/rkab,rkbf->raf/dot_general | solution.py:39
  80.3 0.0 copy-done.4
  80.3 0.8 fusion.5
  81.1 0.1 fusion.15
  81.3 2.5 collective-permute-start.2
  83.8 1.5 collective-permute-start.3
  85.3 18.2 %collective-permute-done.2 = bf16[896,512]{1,0:T(8,128)(2,1)S(1)} collective-permute-done((bf16[896,512]{1,0:T(8,128)(2,1)S(1)}, bf16[896,512]{1,0:T(8,128)(2,1)S(1)}, u32[]{:S(2)}, u32[]{:S(2)}) %collective-permute-start.2) | collective-permute-done | bytes 917536 | tf_op jit(solution)/shard_map/ppermute | solution.py:22
  103.5 23.8 %collective-permute-done.3 = bf16[896,512]{1,0:T(8,128)(2,1)S(1)} collective-permute-done((bf16[896,512]{1,0:T(8,128)(2,1)S(1)}, bf16[896,512]{1,0:T(8,128)(2,1)S(1)}, u32[]{:S(2)}, u32[]{:S(2)}) %collective-permute-start.3) | collective-permute-done | bytes 917536 | tf_op jit(solution)/shard_map/ppermute | solution.py:24
  127.3 1.8 pad_maximum_fusion.1
  129.1 9.5 %gather_fusion.1 = bf16[120,128,512]{2,1,0:T(8,128)(2,1)} fusion(bf16[22,128,512]{2,1,0:T(8,128)(2,1)} %bitcast.66, s32[1024]{0:T(1024)S(1)} %pad_clamp_fusion), kind=kCustom, calls=%fused_computation.1 | custom fusion | bytes 31457760 | tf_op jit(solution)/shard_map/gather | solution.py:38
  138.6 9.0 %bitcast_convert_fusion = bf16[8,512,128]{1,2,0:T(8,128)(2,1)S(1)} fusion(bf16[8,15,128,512]{3,2,1,0:T(8,128)(2,1)} %bitcast.68, bf16[1,8,15,128,128]{4,3,2,1,0:T(8,128)(2,1)} %param.8), kind=kOutput, calls=%fused_computation.12 | convolution fusion | flops 2013790208 | bytes 20709376 | tf_op jit(solution)/shard_map/rkab,rkbf->raf/dot_general | solution.py:39
  147.6 0.0 copy-start.2
  147.7 1.0 copy-done.2
  148.6 1.7 convolution_bitcast_fusion
  150.4 0.0 copy-start.3
  150.4 0.0 all-gather.3.cloned.1.call-update
  150.4 0.0 copy-start.6
  150.4 1.5 multiply_convert_fusion
  151.9 0.0 copy-done.3
  151.9 0.0 copy-done.6
  151.9 1.7 fusion.12
  153.6 193.9 %all-gather.3.cloned.1.call-done = f32[16384,512]{0,1:T(8,128)} async-done(((f32[512,512]{0,1:T(8,128)}), f32[16384,512]{0,1:T(8,128)}) %all-gather.3.cloned.1.call-update) | async-done | bytes 33554448 | tf_op jit(solution)/shard_map/all_gather | solution.py:10
  347.5 32.5 %copy.11 = f32[64,8,32,512]{3,2,1,0:T(8,128)S(1)} copy(f32[64,8,32,512]{3,1,2,0:T(8,128)} %bitcast.70) | data formatting | bytes 67108864
  380.0 0.0 copy-start.1
  380.0 5.4 %bitcast_reduce_fusion = f32[512,512]{0,1:T(8,128)S(1)} fusion(f32[64,8,32,512]{3,2,1,0:T(8,128)S(1)} %copy.11), kind=kLoop, calls=%fused_computation.2 | loop fusion | flops 8126464 | bytes 34603008 | tf_op jit(solution)/shard_map/reduce_sum | solution.py:11
  385.4 1.3 copy.8
  386.7 0.0 copy-done.1
  (2 shorter events, 0.0 us)
Async XLA Ops:
  7.2 1.2 copy-start
  7.2 11.2 %copy-start.5 = (s32[1,8,15]{2,1,0:T(8,128)S(1)}, s32[1,8,15]{2,1,0:T(8,128)}, u32[]{:S(2)}) copy-start(s32[1,8,15]{2,1,0:T(8,128)} %param.7) | copy-start | bytes 1444
  7.2 340.3 %all-gather.3.cloned.1.call-start = ((), (), s32[]{:S(2)}) async-start(), calls=%async_computation | async-start | bytes 34603008 | tf_op jit(solution)/shard_map/all_gather | solution.py:10
  11.2 24.8 %collective-permute-start = (bf16[896,512]{1,0:T(8,128)(2,1)}, bf16[896,512]{1,0:T(8,128)(2,1)}, u32[]{:S(2)}, u32[]{:S(2)}) collective-permute-start(bf16[896,512]{1,0:T(8,128)(2,1)} %get-tuple-element.8), channel_id=1, source_target_pairs={{0,1},{1,2},{2,3},{3,4},{4,5},{5,6},{6,7},{7,8},{8,9},{9,10},{10,1... | collective-permute-start | bytes 2752520 | tf_op jit(solution)/shard_map/ppermute | solution.py:22
  17.1 42.2 %collective-permute-start.1 = (bf16[896,512]{1,0:T(8,128)(2,1)S(1)}, bf16[896,512]{1,0:T(8,128)(2,1)}, u32[]{:S(2)}, u32[]{:S(2)}) collective-permute-start(bf16[896,512]{1,0:T(8,128)(2,1)S(1)} %get-tuple-element.9), channel_id=1, source_target_pairs={{1,0},{2,1},{3,2},{4,3},{5,4},{6,5},{7,6},{8,7},{9,8},{10,9},{11,1... | collective-permute-start | bytes 2752520 | tf_op jit(solution)/shard_map/ppermute | solution.py:24
  72.1 8.2 %copy-start.4 = (bf16[1,1024,512]{2,1,0:T(8,128)(2,1)S(1)}, bf16[1,1024,512]{2,1,0:T(8,128)(2,1)}, u32[]{:S(2)}) copy-start(bf16[1,1024,512]{2,1,0:T(8,128)(2,1)} %param.9) | copy-start | bytes 3145732
  81.3 22.2 %collective-permute-start.2 = (bf16[896,512]{1,0:T(8,128)(2,1)S(1)}, bf16[896,512]{1,0:T(8,128)(2,1)S(1)}, u32[]{:S(2)}, u32[]{:S(2)}) collective-permute-start(bf16[896,512]{1,0:T(8,128)(2,1)S(1)} %get-tuple-element.6), channel_id=1, source_target_pairs={{0,1},{1,2},{2,3},{3,4},{4,5},{5,6},{6,7},{7,8},{8,9},{9,10},{10,1... | collective-permute-start | bytes 2752520 | tf_op jit(solution)/shard_map/ppermute | solution.py:22
  83.8 43.5 %collective-permute-start.3 = (bf16[896,512]{1,0:T(8,128)(2,1)S(1)}, bf16[896,512]{1,0:T(8,128)(2,1)S(1)}, u32[]{:S(2)}, u32[]{:S(2)}) collective-permute-start(bf16[896,512]{1,0:T(8,128)(2,1)S(1)} %get-tuple-element.7), channel_id=1, source_target_pairs={{1,0},{2,1},{3,2},{4,3},{5,4},{6,5},{7,6},{8,7},{9,8},{10,9},{11,1... | collective-permute-start | bytes 2752520 | tf_op jit(solution)/shard_map/ppermute | solution.py:24
  147.6 1.0 copy-start.2
  150.4 1.6 copy-start.3
  150.4 1.5 copy-start.6
  380.0 6.7 %copy-start.1 = (bf16[1,1024,512]{2,1,0:T(8,128)(2,1)S(1)}, bf16[1,1024,512]{2,1,0:T(8,128)(2,1)}, u32[]{:S(2)}) copy-start(bf16[1,1024,512]{2,1,0:T(8,128)(2,1)} %param.5) | copy-start | bytes 3145732
Sparse Core Ops, SparseCore 0:
  150.5 196.9 all-gather.2
